TPU v7x, 256 devices: a whole 4x4x8 slice. The times are simulated.
256 devices in a mesh: lat: 8 (over x, y_hi), lon: 32 (over y_lo, z, core).
Axes of the slice: x: 4, y: 4 (y_hi: 2, y_lo: 2; y = y_hi * 2 + y_lo), z: 8, core: 2. Of those that a mesh axis runs over, the one named last changes fastest.
Arguments:
- tracers: float32 [128, 1440, 1536], P('lat', 'lon'), may hold values from 0.05 to 9, as said below
- winds: float32 [128, 1440, 32], P('lat', 'lon'), may hold values from -0.16 to 0.16
- row_mask: int32 [128], P('lat'), may hold values from 0 to 1, as said below
- coag_rate: float32 [16], replicated, may hold values from 0.05 to 0.3
- growth_rate: float32 [16], replicated, may hold values from 0.05 to 0.3
Outputs:
- updated: float32 [128, 1440, 1536], P('lat', 'lon')
Inputs may be any that keep to these rules, and one draw needn't show every extreme that they name: `tracers`: per cell, mode and level the six channels are M_k = N exp(k mu + k^2 s^2 / 2), k = 0..5, with N in 0.3 to 3, mu in -0.5 to -0.2 and s in 0.25 to 0.4. `row_mask`: 1 on the first K rows (those nearest the pole) and 0 elsewhere, with 16 <= K <= 48.
All inputs are finite; a program needn't handle non-finite values.
Results may differ from a plain program's by a relative error of at most 0.00005.
Values sent between devices are 32-bit elements; how exact they have to be, the bound alone decides.
A program may use at most 128 MiB of HBM per device.

v0:
```python
import math

import jax
import jax.numpy as jnp
from jax import lax
from jax.sharding import Mesh
from jax.sharding import PartitionSpec as P

NLON = 1440
GLOBE_ROWS = 720
LEV = 16
MODES = 16
MOMENTS = 6
LON = ("lon_0", "lon_1", "lon_2")


CUT_COSINE = math.cos(math.pi / 4.0)


def cut_along(array, dim, devices):
    dims = array.shape
    blocks = array.reshape(*dims[:dim], devices, dims[dim] // devices, *dims[dim + 1 :])
    return jnp.moveaxis(blocks, dim, 0)


def in_order(blocks, dim):
    blocks = jnp.moveaxis(blocks, 0, dim)
    dims = blocks.shape
    return blocks.reshape(*dims[:dim], dims[dim] * dims[dim + 1], *dims[dim + 2 :])


def turned_blocks(blocks, axes, sequence):
    inside = blocks.shape[1:]
    out = blocks.reshape(*(lax.axis_size(a) for a in axes), *inside)
    for k in sequence:
        out = lax.all_to_all(out, axes[k], k, k, tiled=True)
    return out.reshape(-1, *inside)


def exchange_by_chip(array, groups, sequence, split_dim, concat_dim):
    devices = lax.axis_size(groups[0]) * lax.axis_size(groups[1])
    blocks = cut_along(array, split_dim, devices)
    return in_order(turned_blocks(blocks, groups, sequence), concat_dim)


def with_halo(array, sides, width, wrap):
    for axis, dim in sides:
        devices, length = (lax.axis_size(axis), array.shape[dim])
        up = [(i, (i + 1) % devices) for i in range(devices if wrap else devices - 1)]
        down = [(j, i) for i, j in up]
        last = lax.slice_in_dim(array, length - width, length, axis=dim)
        initial = lax.slice_in_dim(array, 0, width, axis=dim)
        before = lax.ppermute(last, axis, up)
        after = lax.ppermute(initial, axis, down)
        array = jnp.concatenate([before, array, after], axis=dim)
    return array


def row_angles(places):
    return (-90.0 + 180.0 * (places.astype(jnp.float32) + 0.5) / GLOBE_ROWS) * (math.pi / 180.0)


def damping(angles, length):
    waves = jnp.arange(length // 2 + 1, dtype=jnp.float32)
    sines = jnp.sin(waves * (math.pi / length))
    cosines = jnp.cos(angles)[:, None]
    return cosines / jnp.maximum(CUT_COSINE * sines[None, :], cosines)


def wave_table(amount, length):
    places = jnp.arange(amount, dtype=jnp.int32)
    waves = jnp.arange(length // 2 + 1, dtype=jnp.int32)
    phase = places[:, None] * waves[None, :] % length
    angle = phase.astype(jnp.float32) * (2.0 * math.pi / length)
    return jnp.concatenate([jnp.cos(angle), jnp.sin(angle)], axis=1)


def moment_sources(moments, coag, growth):
    zeroth, first, second, third, fourth, fifth = moments
    alpha_zero = first / zeroth
    sigma_one = second - alpha_zero * first
    sigma_two = third - alpha_zero * second
    sigma_three = fourth - alpha_zero * third
    sigma_four = fifth - alpha_zero * fourth
    alpha_one = sigma_two / sigma_one - first / zeroth
    beta_one = sigma_one / zeroth
    upper_two = sigma_three - alpha_one * sigma_two - beta_one * second
    upper_three = sigma_four - alpha_one * sigma_three - beta_one * third
    alpha_two = upper_three / upper_two - sigma_two / sigma_one
    beta_two = upper_two / sigma_one
    link_one = jnp.sqrt(beta_one)
    link_two = jnp.sqrt(beta_two)
    centre = (alpha_zero + alpha_one + alpha_two) / 3.0
    shift_zero = alpha_zero - centre
    shift_one = alpha_one - centre
    shift_two = alpha_two - centre
    radius = jnp.sqrt(
        (
            shift_zero * shift_zero
            + shift_one * shift_one
            + shift_two * shift_two
            + 2.0 * (beta_one + beta_two)
        )
        / 6.0
    )
    scaled_zero = shift_zero / radius
    scaled_one = shift_one / radius
    scaled_two = shift_two / radius
    ratio_one = beta_one / (radius * radius)
    ratio_two = beta_two / (radius * radius)
    half_det = 0.5 * (scaled_zero * (scaled_one * scaled_two - ratio_two) - ratio_one * scaled_two)
    angle = jnp.arccos(jnp.clip(half_det, -1.0, 1.0)) / 3.0
    top_node = centre + 2.0 * radius * jnp.cos(angle)
    low_node = centre + 2.0 * radius * jnp.cos(angle + 2.0 * math.pi / 3.0)
    mid_node = 3.0 * centre - top_node - low_node
    abscissae = (top_node, mid_node, low_node)
    weights = []
    for node in abscissae:
        poly_one = (node - alpha_zero) / link_one
        poly_two = ((node - alpha_one) * poly_one - link_one) / link_two
        weights.append(zeroth / (1.0 + poly_one * poly_one + poly_two * poly_two))
    volumes = [node * node * node for node in abscissae]
    results = []
    for degree in range(6):
        merged = jnp.zeros_like(zeroth)
        for source in range(3):
            for target in range(3):
                joined = volumes[source] + volumes[target]
                change = (
                    jnp.exp(degree / 3.0 * jnp.log(joined))
                    - abscissae[source] ** degree
                    - abscissae[target] ** degree
                )
                merged = merged + weights[source] * weights[target] * joined * change
        growth_sum = jnp.zeros_like(zeroth)
        if degree > 0:
            for source in range(3):
                growth_sum = growth_sum + weights[source] * abscissae[source] ** (degree - 1) / (
                    1.0 + abscissae[source]
                )
            growth_sum = degree * growth * growth_sum
        results.append(moments[degree] + 0.5 * coag * merged + growth_sum)
    return tuple(results)


def expand_levels(speed, spread):
    band_rows, sector_cols, levels = speed.shape
    flat = speed.reshape(band_rows * sector_cols, levels)
    wide = jnp.dot(
        flat, spread, precision=lax.Precision.HIGHEST, preferred_element_type=jnp.float32
    )
    return wide.reshape(band_rows, sector_cols, spread.shape[1])


def local(tracers, winds, row_mask, coag_rate, growth_rate):
    band_rows, sector_cols, tracer_width = tracers.shape
    wind_width = winds.shape[2]
    total_rows = lax.axis_size("lat") * band_rows
    row_start = lax.axis_index("lat") * band_rows
    global_rows = row_start + jnp.arange(band_rows, dtype=jnp.int32)
    angles = row_angles(global_rows)
    waves = jnp.arange(NLON // 2 + 1, dtype=jnp.int32)
    multiple = jnp.where((waves == 0) | (waves == NLON // 2), 1.0, 2.0) / NLON
    factor = damping(angles, NLON) * multiple[None, :]
    scale = jnp.concatenate([factor, factor], axis=1)
    circles = lax.all_to_all(winds, LON, split_axis=2, concat_axis=1, tiled=True)
    full_table = wave_table(NLON, NLON)
    spectrum = jnp.einsum("rlf,lm->rmf", circles, full_table, precision=lax.Precision.HIGHEST)
    returned = jnp.einsum(
        "rmf,jm->rjf", spectrum * scale[:, :, None], full_table, precision=lax.Precision.HIGHEST
    )
    smooth = exchange_by_chip(returned, (("lon_0", "lon_1"), "lon_2"), (1, 0), 1, 2)
    filtered = jnp.where(row_mask[:, None, None] > 0, smooth, winds)
    padding = (128 - wind_width % 128) % 128
    blank = jnp.zeros((band_rows, sector_cols, padding), jnp.float32)
    combined = jnp.concatenate([tracers, filtered, blank], axis=2)
    sector_ext = with_halo(combined, ((LON, 1),), 1, True)
    band_ext = with_halo(combined, (("lat", 0),), 1, False)
    east_side = sector_ext[:, 2:, :]
    west_side = sector_ext[:, :-2, :]
    north_side = band_ext[2:, :, :]
    south_side = band_ext[:-2, :, :]
    east_value = east_side[:, :, :tracer_width]
    west_value = west_side[:, :, :tracer_width]
    north_value = north_side[:, :, :tracer_width]
    south_value = south_side[:, :, :tracer_width]
    east_edge = east_side[:, :, tracer_width:]
    west_edge = west_side[:, :, tracer_width:]
    north_edge = north_side[:, :, tracer_width:]
    south_edge = south_side[:, :, tracer_width:]
    zonal = filtered[:, :, :LEV]
    merid = filtered[:, :, LEV:]
    east_level = 0.5 * (zonal + east_edge[:, :, :LEV])
    west_level = 0.5 * (west_edge[:, :, :LEV] + zonal)
    north_level = 0.5 * (merid + north_edge[:, :, LEV : 2 * LEV])
    south_level = 0.5 * (south_edge[:, :, LEV : 2 * LEV] + merid)
    channel_level = jnp.arange(tracer_width, dtype=jnp.int32) % LEV
    spread = (channel_level[None, :] == jnp.arange(LEV, dtype=jnp.int32)[:, None]).astype(
        jnp.float32
    )
    east_speed = expand_levels(east_level, spread)
    west_speed = expand_levels(west_level, spread)
    north_speed = expand_levels(north_level, spread)
    south_speed = expand_levels(south_level, spread)
    open_north = (global_rows < total_rows - 1).astype(jnp.float32)[:, None, None]
    open_south = (global_rows > 0).astype(jnp.float32)[:, None, None]
    flux_east = jnp.maximum(east_speed, 0.0) * tracers + jnp.minimum(east_speed, 0.0) * east_value
    flux_west = jnp.maximum(west_speed, 0.0) * west_value + jnp.minimum(west_speed, 0.0) * tracers
    flux_north = (
        jnp.maximum(north_speed, 0.0) * tracers + jnp.minimum(north_speed, 0.0) * north_value
    ) * open_north
    flux_south = (
        jnp.maximum(south_speed, 0.0) * south_value + jnp.minimum(south_speed, 0.0) * tracers
    ) * open_south
    advected = tracers - (flux_east - flux_west) - (flux_north - flux_south)
    block_width = MODES * LEV
    coag = jnp.repeat(coag_rate, LEV)
    growth = jnp.repeat(growth_rate, LEV)
    pieces = tuple(
        (
            advected[:, :, degree * block_width : (degree + 1) * block_width]
            for degree in range(MOMENTS)
        )
    )
    updated = moment_sources(pieces, coag, growth)
    return jnp.concatenate(updated, axis=2)


def solution(mesh):
    split = Mesh(
        mesh.devices.reshape(mesh.shape["lat"], 2, 8, 2), ("lat", "lon_0", "lon_1", "lon_2")
    )
    return jax.shard_map(
        local,
        mesh=split,
        in_specs=(P("lat", LON, None), P("lat", LON, None), P("lat"), P(), P()),
        out_specs=P("lat", LON, None),
        check_vma=False,
    )
```

profile of v0, /device:TPU:3, one launch (start us, length us, event | category | flops | bytes accessed | tf_op | source)
XLA Modules:
  0.0 150.0 jit_solution(9433624216074700869)
XLA Ops:
  0.0 1.1 copy.97
  1.1 0.9 reshape.121
  2.0 10.3 %all-to-all-start = ((f32[32,1,720]{2,1,0:T(1,128)}), f32[32,1,720]{2,1,0:T(1,128)S(1)}, u32[]{:S(2)}, u32[]{:S(2)}) async-start(f32[32,1,720]{2,1,0:T(1,128)} %reshape.121), calls=%async_computation | async-start | bytes 196608 | tf_op jit(solution)/shard_map/all_to_all | solution.py:166
  12.4 0.0 copy-start.1
  12.4 0.0 copy-start.4
  12.4 0.0 copy-start.3
  12.4 19.5 %fusion.20 = (f32[1440,721]{1,0:T(8,128)}, f32[1440,721]{1,0:T(8,128)}) fusion(), kind=kLoop, calls=%fused_computation.27 | loop fusion | flops 9344160 | bytes 8305920 | tf_op jit(solution)/shard_map/sin | solution.py:75
  31.9 0.2 copy.72
  32.3 0.1 broadcast_in_dim.29
  32.4 0.1 mul.938
  32.4 0.1 broadcast_in_dim.30
  32.5 0.1 mul.1017
  32.6 0.1 divide_multiply_fusion
  32.7 0.0 all-to-all-done
  32.7 0.6 broadcast.252
  33.3 0.9 reduce
  34.2 0.2 reshape.122
  34.4 0.1 copy.67
  34.5 0.0 slice-start.2
  34.5 0.2 reshape.114
  34.7 0.0 slice-start.3
  34.7 8.7 %fusion.25 = f32[16,1442]{1,0:T(8,128)S(1)} fusion(f32[16,1440]{1,0:T(8,128)S(1)} %reshape.114, f32[1440,721]{1,0:T(8,128)} %get-tuple-element.29, f32[1440,721]{1,0:T(8,128)} %get-tuple-element.30, f32[16,721]{1,0:T(8,128)S(1)} %divide_multiply_fusion), kind=kOutput, calls=%fused_computation.32 | convolution fusion | flops 400806784 | bytes 8536512 | tf_op jit(solution)/shard_map/rlf,lm->rmf/dot_general | solution.py:168
  43.5 0.0 copy-start.5
  43.5 7.9 %fusion.26 = f32[16,1440,1]{1,0,2:T(8,128)S(1)} fusion(f32[16,1442]{1,0:T(8,128)S(1)} %fusion.25, f32[1440,721]{1,0:T(8,128)S(1)} %bitcast.61, f32[1440,721]{1,0:T(8,128)S(1)} %copy-done), kind=kOutput, calls=%fused_computation.33 | convolution fusion | flops 400760640 | bytes 8490368 | tf_op jit(solution)/shard_map/rmf,jm->rjf/dot_general | solution.py:169
  51.4 0.3 reshape.116
  51.7 0.2 copy.68
  51.9 0.3 reshape.123
  52.2 3.7 %all_to_all.25 = f32[2,1,11520]{2,1,0:T(1,128)S(1)} all-to-all(f32[2,1,11520]{2,1,0:T(1,128)S(1)} %reshape.123), channel_id=1, replica_groups=mesh['lat'=8,'lon_0'=2,'lon_1'=8,'lon_2'=2] {'lon_2'}, dimensions={0} | all-to-all | bytes 184320 | tf_op jit(solution)/shard_map/all_to_all | solution.py:36
  55.9 1.0 reduce.1
  56.8 0.3 reshape.124
  57.1 1.0 reshape.125
  58.2 7.7 %all-to-all-start.2 = ((f32[16,1,1440]{2,1,0:T(1,128)}), f32[16,1,1440]{2,1,0:T(1,128)S(1)}, u32[]{:S(2)}, u32[]{:S(2)}) async-start(f32[16,1,1440]{2,1,0:T(1,128)} %reshape.125), calls=%async_computation.2 | async-start | bytes 196608 | tf_op jit(solution)/shard_map/all_to_all | solution.py:36
  65.9 7.4 %all-to-all-done.2 = f32[16,1,1440]{2,1,0:T(1,128)S(1)} async-done(((f32[16,1,1440]{2,1,0:T(1,128)}), f32[16,1,1440]{2,1,0:T(1,128)S(1)}, u32[]{:S(2)}, u32[]{:S(2)}) %all-to-all-start.2) | async-done | bytes 92192 | tf_op jit(solution)/shard_map/all_to_all | solution.py:36
  73.3 0.9 reduce.2
  74.2 0.3 reshape.126
  74.5 0.3 copy.71
  74.8 0.1 bitcast_select_fusion
  75.0 6.1 %concatenate.28 = f32[16,45,1664]{2,0,1:T(8,128)} concatenate(f32[16,45,1536]{2,0,1:T(8,128)} %param.5, f32[16,45,32]{2,0,1:T(8,128)S(1)} %bitcast_select_fusion, f32[16,45,96]{2,0,1:T(8,128)S(1)} %broadcast_in_dim.28), dimensions={2} | concatenate | bytes 9584640 | tf_op jit(solution)/shard_map/concatenate | solution.py:176
  81.1 1.0 fusion.221
  82.0 1.9 %collective-permute-start = (f32[16,1,1664]{2,0,1:T(8,128)S(1)}, f32[16,1,1664]{2,0,1:T(8,128)S(1)}, u32[]{:S(2)}, u32[]{:S(2)}) collective-permute-start(f32[16,1,1664]{2,0,1:T(8,128)S(1)} %get-tuple-element.17), channel_id=1, source_target_pairs={{1,0},{2,1},{3,2},{4,3},{5,4},{6,5},{7,6},{8,7},{9,8},{10,9},{11,1... | collective-permute-start | bytes 319496 | tf_op jit(solution)/shard_map/ppermute | solution.py:54
  83.9 2.8 %fusion.222 = (f32[1,45,1664]{2,0,1:T(1,128)S(1)}, f32[1,45,1664]{2,0,1:T(1,128)S(1)}) fusion(f32[16,45,1664]{2,0,1:T(8,128)} %concatenate.28), kind=kLoop, calls=%fused_computation.311 | loop fusion | bytes 1198080 | tf_op jit(solution)/shard_map/slice | solution.py:52
  86.7 0.9 collective-permute-start.1
  87.6 4.5 %collective-permute-start.2 = (f32[1,45,1664]{2,0,1:T(1,128)S(1)}, f32[1,45,1664]{2,0,1:T(1,128)S(1)}, u32[]{:S(2)}, u32[]{:S(2)}) collective-permute-start(f32[1,45,1664]{2,0,1:T(1,128)S(1)} %get-tuple-element.19), channel_id=1, source_target_pairs={{32,0},{64,32},{96,64},{128,96},{160,128},{192,160},{224,192},{33,... | collective-permute-start | bytes 898568 | tf_op jit(solution)/shard_map/ppermute | solution.py:54
  92.1 0.0 slice-start
  92.1 0.0 slice-start.1
  92.1 2.8 %collective-permute-start.3 = (f32[1,45,1664]{2,0,1:T(1,128)S(1)}, f32[1,45,1664]{2,0,1:T(1,128)S(1)}, u32[]{:S(2)}, u32[]{:S(2)}) collective-permute-start(f32[1,45,1664]{2,0,1:T(1,128)S(1)} %get-tuple-element.20), channel_id=1, source_target_pairs={{0,32},{32,64},{64,96},{96,128},{128,160},{160,192},{192,224},{1,3... | collective-permute-start | bytes 898568 | tf_op jit(solution)/shard_map/ppermute | solution.py:53
  94.9 0.0 collective-permute-done
  94.9 2.9 %fusion.184 = f32[16,45,1536]{2,0,1:T(8,128)S(1)} fusion(f32[16,1,1664]{2,0,1:T(8,128)S(1)} %collective-permute-done, f32[16,45,1664]{2,0,1:T(8,128)} %concatenate.28, f32[16,45,32]{2,0,1:T(8,128)S(1)} %bitcast_select_fusion, s32[1536]{0:T(1024)S(1)} %add_select_fusion.1), kind=kOutput, calls=%fused_computation.257 | convolution fusion | flops 212395776 | bytes 9420800 | tf_op jit(solution)/shard_map/dot_general | solution.py:149
  97.8 0.0 collective-permute-done.1
  97.8 0.0 slice-start.4
  97.8 1.9 %fusion.179 = f32[16,45,1536]{2,0,1:T(8,128)S(1)} fusion(f32[16,45,1664]{2,0,1:T(8,128)S(1)} %bitcast.59, f32[16,1,1664]{2,0,1:T(8,128)S(1)} %collective-permute-done.1, f32[16,45,32]{2,0,1:T(8,128)S(1)} %bitcast_select_fusion, s32[1536]{0:T(1024)S(1)} %add_select_fusion.1), kind=kOutput, calls=%fused_computation.252 | convolution fusion | flops 212395776 | bytes 9420800 | tf_op jit(solution)/shard_map/dot_general | solution.py:149
  99.7 0.0 slice-start.5
  99.7 7.9 %collective-permute-done.2 = f32[1,45,1664]{2,0,1:T(1,128)S(1)} collective-permute-done((f32[1,45,1664]{2,0,1:T(1,128)S(1)}, f32[1,45,1664]{2,0,1:T(1,128)S(1)}, u32[]{:S(2)}, u32[]{:S(2)}) %collective-permute-start.2) | collective-permute-done | bytes 299552 | tf_op jit(solution)/shard_map/ppermute | solution.py:54
  107.6 4.1 %fusion.174 = f32[16,45,1536]{2,0,1:T(8,128)} fusion(f32[1,45,1664]{2,0,1:T(1,128)S(1)} %collective-permute-done.2, f32[16,45,1664]{2,0,1:T(8,128)S(1)} %bitcast.59, f32[16,45,32]{2,0,1:T(8,128)S(1)} %bitcast_select_fusion, s32[1536]{0:T(1024)S(1)} %add_select_fusion.1), kind=kOutput, calls=%fused_computation.247 | convolution fusion | flops 212395776 | bytes 9613824 | tf_op jit(solution)/shard_map/dot_general | solution.py:149
  111.7 9.5 %fusion.8 = f32[16,45,1536]{2,0,1:T(8,128)S(1)} fusion(f32[16,45,1664]{2,0,1:T(8,128)S(1)} %bitcast.59, f32[1,45,1664]{2,0,1:T(1,128)S(1)} %collective-permute-done.3, f32[1,45,1664]{2,0,1:T(1,128)S(1)} %collective-permute-done.2, f32[16,45,1536]{2,0,1:T(8,128)S(1)} %bitcast.63, f32[16,1,1664]{2,0,1:T(8,128)S(1)} %collective-permute-done.1, ...), kind=kOutput, calls=%fused_computation.11 | convolution fusion | flops 245573376 | bytes 33192448 | tf_op jit(solution)/shard_map/dot_general | solution.py:149
  121.2 0.2 multiply_subtract_fusion.13
  121.5 12.3 %add_dynamic-update-slice_fusion = (f32[16,45,1536]{2,0,1:T(8,128)S(1)}, f32[16,45,256]{2,0,1:T(8,128)S(1)}, f32[16,45,256]{2,0,1:T(8,128)S(1)}, f32[16,45,256]{...) fusion(f32[256]{0:T(256)S(1)} %mul.938, ...), kind=kLoop, calls=%fused_computation.207 | loop fusion | flops 27095040 | bytes 13272064
  133.7 2.7 %fusion.65 = f32[16,45,1536]{2,0,1:T(8,128)S(1)} fusion(f32[16,45,1536]{2,0,1:T(8,128)S(1)} %get-tuple-element.5, f32[16,45,256]{2,0,1:T(8,128)S(1)} %get-tuple-element.13, f32[16,45,256]{2,0,1:T(8,128)S(1)} %get-tuple-element.14, f32[16,45,256]{2,0,1:T(8,128)S(1)} %get-tuple-element.6, f32[16,45,256]{2,0,1:T(8,128)S(1)} %get-tuple-element.10, ...), kind=kLoop, calls=%fused_computation.108 | loop fusion | flops 14929920 | bytes 8849408
  136.4 2.7 %fusion.37 = f32[16,45,1536]{2,0,1:T(8,128)S(1)} fusion(f32[16,45,1536]{2,0,1:T(8,128)S(1)} %fusion.65, f32[16,45,256]{2,0,1:T(8,128)S(1)} %get-tuple-element.13, f32[16,45,256]{2,0,1:T(8,128)S(1)} %get-tuple-element.14, f32[16,45,256]{2,0,1:T(8,128)S(1)} %get-tuple-element.6, f32[16,45,256]{2,0,1:T(8,128)S(1)} %get-tuple-element.10, ...), kind=kLoop, calls=%fused_computation.80 | loop fusion | flops 14929920 | bytes 5900288
  139.1 2.5 %fusion.44 = f32[16,45,1536]{2,0,1:T(8,128)S(1)} fusion(f32[16,45,1536]{2,0,1:T(8,128)S(1)} %fusion.37, f32[16,45,256]{2,0,1:T(8,128)S(1)} %get-tuple-element.6, f32[16,45,256]{2,0,1:T(8,128)S(1)} %get-tuple-element.13, f32[16,45,256]{2,0,1:T(8,128)S(1)} %get-tuple-element.10, f32[16,45,256]{2,0,1:T(8,128)S(1)} %get-tuple-element.8, ...), kind=kLoop, calls=%fused_computation.87 | loop fusion | flops 13824000 | bytes 5900288
  141.7 2.8 %fusion.96 = f32[16,45,1536]{2,0,1:T(8,128)S(1)} fusion(f32[16,45,1536]{2,0,1:T(8,128)S(1)} %fusion.44, f32[16,45,256]{2,0,1:T(8,128)S(1)} %get-tuple-element.8, f32[16,45,256]{2,0,1:T(8,128)S(1)} %get-tuple-element.10, f32[16,45,256]{2,0,1:T(8,128)S(1)} %get-tuple-element.6, f32[16,45,256]{2,0,1:T(8,128)S(1)} %get-tuple-element.13, ...), kind=kLoop, calls=%fused_computation.139 | loop fusion | flops 15482880 | bytes 5900288
  144.4 0.0 copy-start.2
  144.5 2.1 %copy-done.2 = f32[16,45,1536]{2,0,1:T(8,128)} copy-done((f32[16,45,1536]{2,0,1:T(8,128)}, f32[16,45,1536]{2,0,1:T(8,128)S(1)}, u32[]{:S(2)}) %copy-start.2) | copy-done | bytes 4423704
  146.5 3.5 %fusion.111 = f32[16,45,1536]{2,0,1:T(8,128)} fusion(f32[16,45,1536]{2,0,1:T(8,128)} %copy-done.2, f32[16,45,256]{2,0,1:T(8,128)S(1)} %get-tuple-element.8, f32[16,45,256]{2,0,1:T(8,128)S(1)} %get-tuple-element.10, f32[16,45,256]{2,0,1:T(8,128)S(1)} %get-tuple-element.6, f32[16,45,256]{2,0,1:T(8,128)S(1)} %get-tuple-element.14, ...), kind=kLoop, calls=%fused_computation.154 | loop fusion | flops 16035840 | bytes 5900288 | tf_op jit(solution)/shard_map/concatenate | solution.py:226
  (27 shorter events, 0.2 us)
Async XLA Ops:
  2.0 30.7 %all-to-all-start = ((f32[32,1,720]{2,1,0:T(1,128)}), f32[32,1,720]{2,1,0:T(1,128)S(1)}, u32[]{:S(2)}, u32[]{:S(2)}) async-start(f32[32,1,720]{2,1,0:T(1,128)} %reshape.121), calls=%async_computation | async-start | bytes 196608 | tf_op jit(solution)/shard_map/all_to_all | solution.py:166
  12.4 19.6 %copy-start.1 = (f32[16,45,32]{1,2,0:T(8,128)S(1)}, f32[16,45,32]{1,2,0:T(8,128)}, u32[]{:S(2)}) copy-start(f32[16,45,32]{1,2,0:T(8,128)} %param.6) | copy-start | bytes 276484
  12.4 19.9 %copy-start.4 = (f32[16]{0:T(128)S(1)}, f32[16]{0:T(128)}, u32[]{:S(2)}) copy-start(f32[16]{0:T(128)} %param.8) | copy-start | bytes 196
  12.4 20.0 %copy-start.3 = (f32[16]{0:T(128)S(1)}, f32[16]{0:T(128)}, u32[]{:S(2)}) copy-start(f32[16]{0:T(128)} %param.9) | copy-start | bytes 196
  34.5 8.9 %slice-start.2 = ((s8[4423680]{0:T(1024)(128)(4,1)}), s8[229376]{0:T(1024)(128)(4,1)S(1)}, s32[]{:S(2)}) async-start(s8[4423680]{0:T(1024)(128)(4,1)} %bitcast.60), calls=%async_computation.5 | async-start | bytes 458752
  34.7 8.8 %slice-start.3 = ((s8[4423680]{0:T(1024)(128)(4,1)}), s8[4194304]{0:T(1024)(128)(4,1)S(1)}, s32[]{:S(2)}) async-start(s8[4423680]{0:T(1024)(128)(4,1)} %bitcast.60), calls=%async_computation.6 | async-start | bytes 8388608
  34.7 8.8 %copy-start = (f32[1440,721]{1,0:T(8,128)S(1)}, f32[1440,721]{1,0:T(8,128)}, u32[]{:S(2)}) copy-start(f32[1440,721]{1,0:T(8,128)} %get-tuple-element.30) | copy-start | bytes 12458884
  43.5 22.4 %copy-start.5 = (s32[16]{0:T(128)S(1)}, s32[16]{0:T(128)}, u32[]{:S(2)}) copy-start(s32[16]{0:T(128)} %param.7) | copy-start | bytes 196
  58.2 15.2 %all-to-all-start.2 = ((f32[16,1,1440]{2,1,0:T(1,128)}), f32[16,1,1440]{2,1,0:T(1,128)S(1)}, u32[]{:S(2)}, u32[]{:S(2)}) async-start(f32[16,1,1440]{2,1,0:T(1,128)} %reshape.125), calls=%async_computation.2 | async-start | bytes 196608 | tf_op jit(solution)/shard_map/all_to_all | solution.py:36
  82.0 12.9 %collective-permute-start = (f32[16,1,1664]{2,0,1:T(8,128)S(1)}, f32[16,1,1664]{2,0,1:T(8,128)S(1)}, u32[]{:S(2)}, u32[]{:S(2)}) collective-permute-start(f32[16,1,1664]{2,0,1:T(8,128)S(1)} %get-tuple-element.17), channel_id=1, source_target_pairs={{1,0},{2,1},{3,2},{4,3},{5,4},{6,5},{7,6},{8,7},{9,8},{10,9},{11,1... | collective-permute-start | bytes 319496 | tf_op jit(solution)/shard_map/ppermute | solution.py:54
  86.7 11.1 %collective-permute-start.1 = (f32[16,1,1664]{2,0,1:T(8,128)S(1)}, f32[16,1,1664]{2,0,1:T(8,128)S(1)}, u32[]{:S(2)}, u32[]{:S(2)}) collective-permute-start(f32[16,1,1664]{2,0,1:T(8,128)S(1)} %get-tuple-element.18), channel_id=1, source_target_pairs={{0,1},{1,2},{2,3},{3,4},{4,5},{5,6},{6,7},{7,8},{8,9},{9,10},{10,1... | collective-permute-start | bytes 319496 | tf_op jit(solution)/shard_map/ppermute | solution.py:53
  87.6 20.0 %collective-permute-start.2 = (f32[1,45,1664]{2,0,1:T(1,128)S(1)}, f32[1,45,1664]{2,0,1:T(1,128)S(1)}, u32[]{:S(2)}, u32[]{:S(2)}) collective-permute-start(f32[1,45,1664]{2,0,1:T(1,128)S(1)} %get-tuple-element.19), channel_id=1, source_target_pairs={{32,0},{64,32},{96,64},{128,96},{160,128},{192,160},{224,192},{33,... | collective-permute-start | bytes 898568 | tf_op jit(solution)/shard_map/ppermute | solution.py:54
  92.1 5.7 %slice-start = ((s8[4792320]{0:T(1024)(128)(4,1)}), s8[4194304]{0:T(1024)(128)(4,1)S(1)}, s32[]{:S(2)}) async-start(s8[4792320]{0:T(1024)(128)(4,1)} %bitcast.58), calls=%async_computation.3 | async-start | bytes 8388608
  92.1 5.7 %slice-start.1 = ((s8[4792320]{0:T(1024)(128)(4,1)}), s8[598016]{0:T(1024)(128)(4,1)S(1)}, s32[]{:S(2)}) async-start(s8[4792320]{0:T(1024)(128)(4,1)} %bitcast.58), calls=%async_computation.4 | async-start | bytes 1196032
  92.1 19.6 %collective-permute-start.3 = (f32[1,45,1664]{2,0,1:T(1,128)S(1)}, f32[1,45,1664]{2,0,1:T(1,128)S(1)}, u32[]{:S(2)}, u32[]{:S(2)}) collective-permute-start(f32[1,45,1664]{2,0,1:T(1,128)S(1)} %get-tuple-element.20), channel_id=1, source_target_pairs={{0,32},{32,64},{64,96},{96,128},{128,160},{160,192},{192,224},{1,3... | collective-permute-start | bytes 898568 | tf_op jit(solution)/shard_map/ppermute | solution.py:53
  97.8 13.9 %slice-start.4 = ((s8[4423680]{0:T(1024)(128)(4,1)}), s8[4194304]{0:T(1024)(128)(4,1)S(1)}, s32[]{:S(2)}) async-start(s8[4423680]{0:T(1024)(128)(4,1)} %bitcast.62), calls=%async_computation.7 | async-start | bytes 8388608
  99.7 12.0 %slice-start.5 = ((s8[4423680]{0:T(1024)(128)(4,1)}), s8[229376]{0:T(1024)(128)(4,1)S(1)}, s32[]{:S(2)}) async-start(s8[4423680]{0:T(1024)(128)(4,1)} %bitcast.62), calls=%async_computation.8 | async-start | bytes 458752
  144.4 2.1 %copy-start.2 = (f32[16,45,1536]{2,0,1:T(8,128)}, f32[16,45,1536]{2,0,1:T(8,128)S(1)}, u32[]{:S(2)}) copy-start(f32[16,45,1536]{2,0,1:T(8,128)S(1)} %fusion.96) | copy-start | bytes 13271044
where the time goes:
time: 151 us; the launch traced here: 150 us
  other arithmetic  49.2 us (33%)
  matrix products  34.9 us (23%)
  starting transfers between devices  28.1 us (19%)
  local copies, waits for them, and re-layouts  18.3 us (12%)
  waiting for transfers between devices  15.3 us (10%)
  blocking collectives  3.67 us (2%)
    unnamed x8, other arithmetic  22.9 us
    sin x1, other arithmetic, wave_table(): return jnp.concatenate([jnp.cos(angle), jnp.sin(angle)], axis=1)  19.5 us
    dot_general x4, matrix products, expand_levels(): jnp.dot(flat, spread, precision=lax.Precision.HIGHEST, preferred_element_...  18.3 us
    all_to_all x1, starting transfers between devices, local(): lax.all_to_all(winds, LON, split_axis=2, concat_axis=1, tiled=True)  10.3 us
    dot_general x1, matrix products, local(): jnp.einsum('rlf,lm->rmf', circles, full_table, precision=lax.Precision.HI...  8.73 us
    ppermute x2, waiting for transfers between devices, with_halo(): after = lax.ppermute(initial, axis, down)  7.89 us
    dot_general x1, matrix products, local(): jnp.einsum('rmf,jm->rjf', spectrum * scale[:, :, None], full_table, preci...  7.86 us
    all_to_all x1, starting transfers between devices, turned_blocks(): out = lax.all_to_all(out, axes[k], k, k, tiled=True)  7.74 us
  transfers between devices with their start and end apart: 6, of which 2 were waited for; matrix products, arithmetic and copies ran while one was open for 21% of the time, Pallas kernels for 0%

commit v1 on v0

v1 whole, which is shorter than its diff:
```python
import functools
import math

import jax
import jax.numpy as jnp
import numpy as np
from jax import lax
from jax.experimental import pallas as pl
from jax.experimental.pallas import tpu as pltpu
from jax.sharding import PartitionSpec as P

NLON = 1440
GLOBE_ROWS = 720
LEV = 16
MODES = 16
MOMENTS = 6
FILTER_ROWS = 48
MESH = pl.DeviceIdType.MESH

POLY = (
    0.5000000260258313,
    0.577346917369578,
    -0.11103851124670026,
    0.052841409139758516,
    -0.03023539756350864,
    0.016047280362516254,
    -0.0060893456734267045,
    0.0011276362373084019,
)


def filter_lines(sectors, cols):
    rows = np.arange(FILTER_ROWS)
    angles = (-90.0 + 180.0 * (rows + 0.5) / GLOBE_ROWS) * (math.pi / 180.0)
    cosines = np.cos(angles)[:, None]
    sines = np.sin(np.arange(NLON // 2 + 1) * (math.pi / NLON))[None, :]
    factor = cosines / np.maximum(math.cos(math.pi / 4.0) * sines, cosines)
    kernel = np.fft.irfft(factor, n=NLON, axis=1)
    lane = np.arange(128)
    shift = np.where(lane < 64, lane, lane - 128)
    place = (cols * np.arange(sectors)[:, None] - 1 + shift[None, :]) % NLON
    return kernel[:, place].astype(np.float32)


def split_two(x):
    high = x.astype(jnp.bfloat16)
    return high, (x - high.astype(jnp.float32)).astype(jnp.bfloat16)


def nodes_of(moments):
    m0, m1, m2, m3, m4, m5 = moments
    inv0 = 1.0 / m0
    a0 = m1 * inv0
    s1 = m2 - a0 * m1
    s2 = m3 - a0 * m2
    s3 = m4 - a0 * m3
    s4 = m5 - a0 * m4
    inv1 = 1.0 / s1
    r21 = s2 * inv1
    a1 = r21 - a0
    b1 = s1 * inv0
    t2 = s3 - a1 * s2 - b1 * m2
    t3 = s4 - a1 * s3 - b1 * m3
    r32 = t3 * (1.0 / t2)
    a2 = r32 - r21
    b2 = t2 * inv1
    c = r32 * (1.0 / 3.0)
    g0, g1, g2 = a0 - c, a1 - c, a2 - c
    p2 = (g0 * g0 + g1 * g1 + g2 * g2) * (1.0 / 6.0) + (b1 + b2) * (1.0 / 3.0)
    inv_p = lax.rsqrt(p2)
    p = p2 * inv_p
    det = g0 * (g1 * g2 - b2) - b1 * g2
    h = jnp.clip((0.5 * det) * (inv_p * inv_p * inv_p), -1.0, 1.0)
    u = jnp.sqrt(0.5 + 0.5 * h)
    y = POLY[-1] * u + POLY[-2]
    for coef in POLY[-3::-1]:
        y = y * u + coef
    s = jnp.sqrt(jnp.maximum(0.75 - 0.75 * (y * y), 0.0))
    py, ps = p * y, p * s
    q = c - py
    return (c + 2.0 * py, q + 2.0 * ps, q - 2.0 * ps), (a0, a1, b1, b2, t2)


def moment_sources(moments, half_coag, growth):
    xs, (a0, a1, b1, b2, t2) = nodes_of(moments)
    ws, hs = [], []
    for x in xs:
        y = x - a0
        z = (x - a1) * y - b1
        den = b2 * (b1 + y * y) + z * z
        above = 1.0 + x
        share = t2 / (den * above)
        ws.append(share * above)
        hs.append(share * growth)
    vs = [x * x * x for x in xs]
    cw = [w * half_coag for w in ws]
    dia = [cw[i] * ws[i] * vs[i] for i in range(3)]
    off, roots = [], []
    for i, j in ((0, 1), (0, 2), (1, 2)):
        joined = vs[i] + vs[j]
        roots.append(jnp.exp(jnp.log(joined) * (1.0 / 3.0)))
        off.append(2.0 * cw[i] * ws[j] * joined)
    ends = [off[0] + off[1], off[0] + off[2], off[1] + off[2]]
    out = [moments[0] - (2.0 * (dia[0] + dia[1] + dia[2]) + (off[0] + off[1] + off[2]))]
    ax = [dia[i] * xs[i] for i in range(3)]
    ex = [ends[i] * xs[i] for i in range(3)]
    for k in range(1, MOMENTS):
        twin = 2.0 * 2.0 ** (k / 3.0) - 4.0
        off = [off[i] * roots[i] for i in range(3)]
        total = moments[k] + (off[0] + off[1] + off[2])
        terms = [twin * ax[i] - ex[i] + float(k) * hs[i] for i in range(3)]
        out.append(total + (terms[0] + terms[1] + terms[2]))
        if k < MOMENTS - 1:
            ax = [ax[i] * xs[i] for i in range(3)]
            ex = [ex[i] * xs[i] for i in range(3)]
            hs = [hs[i] * xs[i] for i in range(3)]
    return out


def kernel(
    bands, sectors, lines_ref, mask_ref, coag_ref, growth_ref, winds_ref, tracers_ref, out_ref,
    line_buf, wsend, wrecv, fsend, frecv, wide_h, wide_l, table_h, table_l, turn, coefs, rates,
    tbuf, obuf, south_buf, north_buf,
    line_sem, load_sem, store_sem, w_send, w_recv, f_send, f_recv, edge_send, edge_recv, v_send, v_recv,
):
    band, me = lax.axis_index("lat"), lax.axis_index("lon")
    north, south = lax.rem(band + 1, bands), lax.rem(band + bands - 1, bands)
    east, west = lax.rem(me + 1, sectors), lax.rem(me + sectors - 1, sectors)
    rows, channels, cols = winds_ref.shape
    width = tracers_ref.shape[-1]
    octets = rows // 8
    lane = lax.broadcasted_iota(jnp.int32, (8, 128), 1)
    sub = lax.broadcasted_iota(jnp.int32, (8, 128), 0)
    low = lane < 64

    barrier = pltpu.get_barrier_semaphore()

    def greet(k, carry):
        pl.semaphore_signal(barrier, inc=1, device_id=(band, lax.rem(me + k, sectors)), device_id_type=MESH)
        return carry

    lax.fori_loop(1, sectors, greet, 0)
    for other in (north, south):
        pl.semaphore_signal(barrier, inc=1, device_id=(other, me), device_id_type=MESH)

    unit_row = lax.div(me, 2)
    line = jnp.minimum(band * rows + unit_row, FILTER_ROWS - 1)
    line_copy = pltpu.make_async_copy(lines_ref.at[line], line_buf, line_sem)
    line_copy.start()
    load = pltpu.make_async_copy(tracers_ref, tbuf.at[pl.ds(1, cols)], load_sem)
    load.start()

    for unit in range(2 * rows):
        wsend[unit] = jnp.zeros((8, 128), jnp.float32)
        for g in range(2):
            start = 16 * (unit % 2) + 8 * g
            wsend[unit, :, 64 * g : 64 * g + cols] = winds_ref[unit // 2, start : start + 8, :]
    for half in range(2):
        c = jnp.zeros((8, 128), jnp.float32)
        g = jnp.zeros((8, 128), jnp.float32)
        for mode in range(8):
            here = lax.div(lane, LEV) == mode
            c = jnp.where(here, 0.5 * coag_ref[8 * half + mode], c)
            g = jnp.where(here, growth_ref[8 * half + mode], g)
        rates[0, half] = c
        rates[1, half] = g

    line_copy.wait()
    filtered = mask_ref[unit_row] > 0
    for k in range(sectors):
        parts = []
        for side in range(2):
            e = (side - k) % sectors
            values = line_buf[e : e + 1, :]
            unit_line = jnp.zeros((1, 128), jnp.float32)
            for x in range(128):
                if (cols * e - 1 + (x if x < 64 else x - 128)) % NLON == 0:
                    unit_line = jnp.where(lax.broadcasted_iota(jnp.int32, (1, 128), 1) == x, 1.0, unit_line)
            values = jnp.where(filtered, values, unit_line)
            parts.append(pltpu.roll(jnp.broadcast_to(values, (64, 128)), 64 * side, 1, stride=1, stride_axis=0))
        left = lax.broadcasted_iota(jnp.int32, (64, 128), 1) < 64
        high, rest = split_two(jnp.where(left, parts[0], parts[1]))
        table_h[64 * k : 64 * k + 64, :] = high
        table_l[64 * k : 64 * k + 64, :] = rest

    pl.semaphore_wait(barrier, sectors + 1)

    def wind_copy(k):
        other = lax.rem(me + k, sectors)
        return pltpu.make_async_remote_copy(
            src_ref=wsend.at[other], dst_ref=wrecv.at[me], send_sem=w_send.at[other], recv_sem=w_recv.at[me],
            device_id=(band, other), device_id_type=MESH,
        )

    def wind_start(k, carry):
        wind_copy(k).start()
        return carry

    lax.fori_loop(1, sectors, wind_start, 0)
    wrecv[me] = wsend[me]

    edges = [
        pltpu.make_async_remote_copy(
            src_ref=tracers_ref.at[cols - 1], dst_ref=tbuf.at[0], send_sem=edge_send.at[0], recv_sem=edge_recv.at[0],
            device_id=(band, east), device_id_type=MESH,
        ),
        pltpu.make_async_remote_copy(
            src_ref=tracers_ref.at[0], dst_ref=tbuf.at[cols + 1], send_sem=edge_send.at[1], recv_sem=edge_recv.at[1],
            device_id=(band, west), device_id_type=MESH,
        ),
        pltpu.make_async_remote_copy(
            src_ref=tracers_ref.at[:, pl.ds(rows - 1, 1), :], dst_ref=south_buf, send_sem=edge_send.at[2],
            recv_sem=edge_recv.at[2], device_id=(north, me), device_id_type=MESH,
        ),
        pltpu.make_async_remote_copy(
            src_ref=tracers_ref.at[:, pl.ds(0, 1), :], dst_ref=north_buf, send_sem=edge_send.at[3],
            recv_sem=edge_recv.at[3], device_id=(south, me), device_id_type=MESH,
        ),
    ]
    for copy in edges:
        copy.start()

    def wind_wait(k, carry):
        other = lax.rem(me + k, sectors)
        pltpu.make_async_remote_copy(
            src_ref=wsend.at[me], dst_ref=wrecv.at[other], send_sem=w_send.at[other], recv_sem=w_recv.at[other],
            device_id=(band, other), device_id_type=MESH,
        ).wait_recv()
        return carry

    lax.fori_loop(1, sectors, wind_wait, 0)

    pairs = sectors // 2
    for q in range(pairs):
        one, two = wrecv[2 * q], wrecv[2 * q + 1]
        block = jnp.concatenate(
            [jnp.where(low, one, pltpu.roll(two, 64, 1)), jnp.where(low, pltpu.roll(one, 64, 1), two)], axis=0
        )
        high, rest = split_two(block)
        for p in range(pairs):
            at = 128 * ((q - p) % pairs)
            wide_h[16 * p : 16 * p + 16, at : at + 128] = high
            wide_l[16 * p : 16 * p + 16, at : at + 128] = rest
    dot = functools.partial(jnp.dot, preferred_element_type=jnp.float32)
    smooth = dot(wide_h[...], table_h[...]) + (dot(wide_l[...], table_h[...]) + dot(wide_h[...], table_l[...]))
    for p in range(pairs):
        one, two = smooth[16 * p : 16 * p + 8, :], smooth[16 * p + 8 : 16 * p + 16, :]
        fsend[2 * p] = jnp.where(low, one, pltpu.roll(two, 64, 1))
        fsend[2 * p + 1] = jnp.where(low, pltpu.roll(one, 64, 1), two)

    def back_start(k, carry):
        other = lax.rem(me + k, sectors)
        pltpu.make_async_remote_copy(
            src_ref=fsend.at[other], dst_ref=frecv.at[me], send_sem=f_send.at[other], recv_sem=f_recv.at[me],
            device_id=(band, other), device_id_type=MESH,
        ).start()
        return carry

    lax.fori_loop(1, sectors, back_start, 0)
    frecv[me] = fsend[me]

    def back_wait(k, carry):
        other = lax.rem(me + k, sectors)
        pltpu.make_async_remote_copy(
            src_ref=fsend.at[me], dst_ref=frecv.at[other], send_sem=f_send.at[other], recv_sem=f_recv.at[other],
            device_id=(band, other), device_id_type=MESH,
        ).wait_recv()
        return carry

    lax.fori_loop(1, sectors, back_wait, 0)

    units = 2 * rows
    to_north = pltpu.make_async_remote_copy(
        src_ref=frecv.at[units - 1], dst_ref=frecv.at[units], send_sem=v_send.at[0], recv_sem=v_recv.at[0],
        device_id=(north, me), device_id_type=MESH,
    )
    to_south = pltpu.make_async_remote_copy(
        src_ref=frecv.at[1], dst_ref=frecv.at[units + 1], send_sem=v_send.at[1], recv_sem=v_recv.at[1],
        device_id=(south, me), device_id_type=MESH,
    )
    to_north.start()
    to_south.start()
    to_north.wait()
    to_south.wait()

    zero = jnp.zeros((8, 128), jnp.float32)
    merid = [frecv[units]] + [frecv[2 * r + 1] for r in range(rows)] + [frecv[units + 1]]
    merid = [pltpu.roll(m, 127, 1) for m in merid]
    faces = [0.5 * (merid[r] + merid[r + 1]) for r in range(rows + 1)]
    faces[0] = jnp.where(band == 0, 0.0, faces[0])
    faces[rows] = jnp.where(band == bands - 1, 0.0, faces[rows])
    ahead = [jnp.maximum(f, 0.0) for f in faces]
    back = [jnp.minimum(f, 0.0) for f in faces]
    for r in range(rows):
        u = frecv[2 * r]
        face = 0.5 * (u + pltpu.roll(u, 127, 1))
        west_p, west_m = jnp.maximum(face, 0.0), jnp.minimum(face, 0.0)
        face = pltpu.roll(face, 127, 1)
        east_p, east_m = jnp.maximum(face, 0.0), jnp.minimum(face, 0.0)
        centre = 1.0 - (east_p - west_m) - (ahead[r + 1] - back[r])
        for n, (a, b) in enumerate(((centre, -east_m), (west_p, -back[r + 1]), (ahead[r], zero))):
            at = 16 * (r % 8)
            turn[n, r // 8, at : at + 8, :] = jnp.where(low, a, pltpu.roll(b, 64, 1))
            turn[n, r // 8, at + 8 : at + 16, :] = jnp.where(low, pltpu.roll(a, 64, 1), b)
    for n in range(3):
        for octet in range(octets):
            coefs[n, octet] = turn[n, octet].T

    load.wait()
    for copy in edges:
        copy.wait()

    own = lax.div(lane, LEV) == sub

    def expand(n, octet, place):
        x = coefs[n, octet, pl.ds(place, 8, stride=0), :]
        x = jnp.where(own, x, 0.0)
        for turnby in (64, 32, 16):
            x = x + pltpu.roll(x, turnby, 1)
        return x

    modes_width = width // MOMENTS

    def column(j, carry):
        places = [(0, j), (0, 64 + j), (1, j), (1, 64 + j), (2, j)]
        stencil = [[expand(n, octet, place) for n, place in places] for octet in range(octets)]
        for part in range(modes_width // 128):
            advected = [[] for _ in range(octets)]
            for k in range(MOMENTS):
                lanes = pl.ds(k * modes_width + part * 128, 128)
                q = [tbuf[j + 1, 8 * o : 8 * o + 8, lanes] for o in range(octets)]
                north_row = jnp.broadcast_to(north_buf[j, :, lanes], (8, 128))
                south_row = jnp.broadcast_to(south_buf[j, :, lanes], (8, 128))
                down = [pltpu.roll(a, 7, 0) for a in q] + [north_row]
                up = [south_row] + [pltpu.roll(a, 1, 0) for a in q]
                for o in range(octets):
                    c, ce, cw, cn, cs = stencil[o]
                    above = jnp.where(sub < 7, down[o], down[o + 1])
                    below = jnp.where(sub > 0, up[o + 1], up[o])
                    octet_rows = pl.ds(8 * o, 8)
                    value = c * q[o] + ce * tbuf[j + 2, octet_rows, lanes] + cw * tbuf[j, octet_rows, lanes]
                    advected[o].append(value + cn * above + cs * below)
            for o in range(octets):
                updated = moment_sources(advected[o], rates[0, part], rates[1, part])
                for k in range(MOMENTS):
                    obuf[j, 8 * o : 8 * o + 8, pl.ds(k * modes_width + part * 128, 128)] = updated[k]
        pltpu.make_async_copy(obuf.at[j], out_ref.at[j], store_sem.at[j]).start()
        return carry

    lax.fori_loop(0, cols, column, 0)

    def store_wait(j, carry):
        pltpu.make_async_copy(obuf.at[j], out_ref.at[j], store_sem.at[j]).wait()
        return carry

    lax.fori_loop(0, cols, store_wait, 0)

    def send_wait(k, carry):
        other = lax.rem(me + k, sectors)
        wind_copy(k).wait_send()
        pltpu.make_async_remote_copy(
            src_ref=fsend.at[other], dst_ref=frecv.at[me], send_sem=f_send.at[other], recv_sem=f_recv.at[me],
            device_id=(band, other), device_id_type=MESH,
        ).wait_send()
        return carry

    lax.fori_loop(1, sectors, send_wait, 0)


def local(bands, sectors, tracers, winds, row_mask, coag_rate, growth_rate):
    rows, cols, width = tracers.shape
    lines = jnp.asarray(filter_lines(sectors, cols))
    f32, bf16 = jnp.float32, jnp.bfloat16
    dma = pltpu.SemaphoreType.DMA
    anywhere = pl.BlockSpec(memory_space=pl.ANY)
    scalars = pl.BlockSpec(memory_space=pltpu.SMEM)
    out = pl.pallas_call(
        functools.partial(kernel, bands, sectors),
        out_shape=jax.ShapeDtypeStruct((cols, rows, width), f32),
        in_specs=[anywhere, scalars, scalars, scalars, pl.BlockSpec(memory_space=pltpu.VMEM), anywhere],
        out_specs=anywhere,
        scratch_shapes=[
            pltpu.VMEM((sectors, 128), f32),
            pltpu.VMEM((sectors, 8, 128), f32),
            pltpu.VMEM((sectors, 8, 128), f32),
            pltpu.VMEM((sectors, 8, 128), f32),
            pltpu.VMEM((sectors + 2, 8, 128), f32),
            pltpu.VMEM((8 * sectors, 64 * sectors), bf16),
            pltpu.VMEM((8 * sectors, 64 * sectors), bf16),
            pltpu.VMEM((64 * sectors, 128), bf16),
            pltpu.VMEM((64 * sectors, 128), bf16),
            pltpu.VMEM((3, rows // 8, 128, 128), f32),
            pltpu.VMEM((3, rows // 8, 128, 128), f32),
            pltpu.VMEM((2, 2, 8, 128), f32),
            pltpu.VMEM((cols + 2, rows, width), f32),
            pltpu.VMEM((cols, rows, width), f32),
            pltpu.VMEM((cols, 1, width), f32),
            pltpu.VMEM((cols, 1, width), f32),
            dma, dma, dma((cols,)),
            dma((sectors,)), dma((sectors,)), dma((sectors,)), dma((sectors,)),
            dma((4,)), dma((4,)), dma((2,)), dma((2,)),
        ],
        compiler_params=pltpu.CompilerParams(collective_id=0, has_side_effects=True),
        name="transport",
    )(lines, row_mask, coag_rate, growth_rate, jnp.transpose(winds, (0, 2, 1)), jnp.transpose(tracers, (1, 0, 2)))
    return jnp.transpose(out, (1, 0, 2))


def solution(mesh):
    bands, sectors = mesh.shape["lat"], mesh.shape["lon"]
    return jax.shard_map(
        functools.partial(local, bands, sectors),
        mesh=mesh,
        in_specs=(P("lat", "lon", None), P("lat", "lon", None), P("lat"), P(), P()),
        out_specs=P("lat", "lon", None),
        check_vma=False,
    )
```

time: 151 us -> 63 us (0.42)
  the two profiles are of different devices: /device:TPU:3 before, /device:TPU:1 now
where the time goes in v1:
time: 63 us; the launch traced here: 62.9 us
  Pallas kernels  58 us (92%)
  local copies, waits for them, and re-layouts  4.88 us (8%)
    pallas_call x1, Pallas kernels, local(): pl.pallas_call(functools.partial(kernel, bands, sectors), out_shape=jax.S...  58 us
    unnamed x1, local copies, waits for them, and re-layouts  4.88 us

profile of v1, /device:TPU:1, one launch (start us, length us, event | category | flops | bytes accessed | tf_op | source)
XLA Modules:
  0.0 62.9 jit_solution(10361439989302478645)
XLA Ops:
  0.0 58.0 %transport.1 = f32[45,16,1536]{2,1,0:T(8,128)} custom-call(f32[48,32,128]{2,1,0:T(8,128)} %constant.2.clone.lines_ref, s32[16]{0:T(128)} %mask_ref.1, f32[16]{0:T(128)} %coag_ref.1, f32[16]{0:T(128)} %growth_ref.1, f32[16,32,45]{2,1,0:T(8,128)} %bitcast.5, f32[45,16,1536]{2,1,0:T(8,128)} %bitcast.4), custom_call_target="tpu_custom_call" | custom-call | tf_op jit(solution)/shard_map/transport/pallas_call | solution.py:377
  58.0 4.9 %copy.8 = f32[16,45,1536]{2,0,1:T(8,128)} copy(f32[16,45,1536]{2,0,1:T(8,128)} %bitcast.3) | data formatting | bytes 8847360

commit v2 on v1

--- a/solution.py
+++ b/solution.py
@@ -15,6 +15,7 @@
 MODES = 16
 MOMENTS = 6
 FILTER_ROWS = 48
+GROUPS = 5
 MESH = pl.DeviceIdType.MESH
 
 POLY = (
@@ -47,7 +48,11 @@
     return high, (x - high.astype(jnp.float32)).astype(jnp.bfloat16)
 
 
-def nodes_of(moments):
+def positive_root(x):
+    return x * lax.rsqrt(x)
+
+
+def moment_sources(moments, coag, growth):
     m0, m1, m2, m3, m4, m5 = moments
     inv0 = 1.0 / m0
     a0 = m1 * inv0
@@ -61,67 +66,71 @@
     b1 = s1 * inv0
     t2 = s3 - a1 * s2 - b1 * m2
     t3 = s4 - a1 * s3 - b1 * m3
-    r32 = t3 * (1.0 / t2)
-    a2 = r32 - r21
+    a2 = t3 * (1.0 / t2) - r21
     b2 = t2 * inv1
-    c = r32 * (1.0 / 3.0)
-    g0, g1, g2 = a0 - c, a1 - c, a2 - c
-    p2 = (g0 * g0 + g1 * g1 + g2 * g2) * (1.0 / 6.0) + (b1 + b2) * (1.0 / 3.0)
+    d1, d2 = a1 - a0, a2 - a0
+    c = (d1 + d2) * (1.0 / 3.0)
+    e2 = d1 * d2 - (b1 + b2)
+    cc = c * c
+    p2 = cc - (1.0 / 3.0) * e2
     inv_p = lax.rsqrt(p2)
     p = p2 * inv_p
-    det = g0 * (g1 * g2 - b2) - b1 * g2
-    h = jnp.clip((0.5 * det) * (inv_p * inv_p * inv_p), -1.0, 1.0)
-    u = jnp.sqrt(0.5 + 0.5 * h)
-    y = POLY[-1] * u + POLY[-2]
+    half_h = c * (0.5 * cc - 0.25 * e2) - 0.25 * (b1 * d2)
+    half_h = half_h * (inv_p * (inv_p * inv_p))
+    u = positive_root(jnp.clip(0.5 + half_h, 1e-30, 1.0))
+    cosine = POLY[-1] * u + POLY[-2]
     for coef in POLY[-3::-1]:
-        y = y * u + coef
-    s = jnp.sqrt(jnp.maximum(0.75 - 0.75 * (y * y), 0.0))
-    py, ps = p * y, p * s
-    q = c - py
-    return (c + 2.0 * py, q + 2.0 * ps, q - 2.0 * ps), (a0, a1, b1, b2, t2)
-
-
-def moment_sources(moments, half_coag, growth):
-    xs, (a0, a1, b1, b2, t2) = nodes_of(moments)
-    ws, hs = [], []
-    for x in xs:
-        y = x - a0
-        z = (x - a1) * y - b1
-        den = b2 * (b1 + y * y) + z * z
-        above = 1.0 + x
-        share = t2 / (den * above)
+        cosine = cosine * u + coef
+    sine = positive_root(jnp.maximum(1.0 - cosine * cosine, 1e-30))
+    along, across = p * cosine, (math.sqrt(3.0) * p) * sine
+    rest = c - along
+    ys = (c + (along + along), rest + across, rest - across)
+    xs = [y + a0 for y in ys]
+    gaps = (ys[0] - ys[1], ys[0] - ys[2], ys[1] - ys[2])
+    dens = (gaps[0] * gaps[1], -gaps[0] * gaps[2], gaps[1] * gaps[2])
+    ws, shares = [], []
+    for i, j, k in ((0, 1, 2), (1, 0, 2), (2, 0, 1)):
+        above = 1.0 + xs[i]
+        share = (s1 + m0 * (ys[j] * ys[k])) / (dens[i] * above)
         ws.append(share * above)
-        hs.append(share * growth)
+        shares.append(share)
     vs = [x * x * x for x in xs]
-    cw = [w * half_coag for w in ws]
-    dia = [cw[i] * ws[i] * vs[i] for i in range(3)]
-    off, roots = [], []
+    cw = [w * coag for w in ws]
+    wv = [ws[i] * vs[i] for i in range(3)]
+    diag = [cw[i] * wv[i] for i in range(3)]
+    q7 = [wv[i] * (vs[i] * xs[i]) for i in range(3)]
+    q8 = [q7[i] * xs[i] for i in range(3)]
+    higher = (m3, m4, m5, None, q7[0] + q7[1] + q7[2], q8[0] + q8[1] + q8[2])
+    pairs, roots, joins = [], [], []
     for i, j in ((0, 1), (0, 2), (1, 2)):
         joined = vs[i] + vs[j]
-        roots.append(jnp.exp(jnp.log(joined) * (1.0 / 3.0)))
-        off.append(2.0 * cw[i] * ws[j] * joined)
-    ends = [off[0] + off[1], off[0] + off[2], off[1] + off[2]]
-    out = [moments[0] - (2.0 * (dia[0] + dia[1] + dia[2]) + (off[0] + off[1] + off[2]))]
-    ax = [dia[i] * xs[i] for i in range(3)]
-    ex = [ends[i] * xs[i] for i in range(3)]
+        roots.append(jnp.exp2(jnp.log(joined) * (math.log2(math.e) / 3.0)))
+        pairs.append(cw[i] * ws[j] * joined)
+        joins.append(joined)
+    cm0, cm3 = coag * m0, coag * m3
+    out = [m0 - cm0 * m3]
+    grown = shares[0] + shares[1] + shares[2]
+    first = pairs
     for k in range(1, MOMENTS):
-        twin = 2.0 * 2.0 ** (k / 3.0) - 4.0
-        off = [off[i] * roots[i] for i in range(3)]
-        total = moments[k] + (off[0] + off[1] + off[2])
-        terms = [twin * ax[i] - ex[i] + float(k) * hs[i] for i in range(3)]
-        out.append(total + (terms[0] + terms[1] + terms[2]))
-        if k < MOMENTS - 1:
-            ax = [ax[i] * xs[i] for i in range(3)]
-            ex = [ex[i] * xs[i] for i in range(3)]
-            hs = [hs[i] * xs[i] for i in range(3)]
+        pairs = [pairs[i] * roots[i] for i in range(3)]
+        diag = [diag[i] * xs[i] for i in range(3)]
+        total = moments[k] + (float(k) * growth) * grown
+        grown = moments[k - 1] - grown
+        if k == 3:
+            left = [pairs[i] - first[i] * joins[i] for i in range(3)]
+            total = total + (left[0] + left[1] + left[2])
+        else:
+            total = total + (pairs[0] + pairs[1] + pairs[2]) - (cm0 * higher[k] + cm3 * moments[k])
+            total = total + 2.0 ** (k / 3.0) * (diag[0] + diag[1] + diag[2])
+        out.append(total)
     return out
 
 
 def kernel(
     bands, sectors, lines_ref, mask_ref, coag_ref, growth_ref, winds_ref, tracers_ref, out_ref,
-    line_buf, wsend, wrecv, fsend, frecv, wide_h, wide_l, table_h, table_l, turn, coefs, rates,
-    tbuf, obuf, south_buf, north_buf,
-    line_sem, load_sem, store_sem, w_send, w_recv, f_send, f_recv, edge_send, edge_recv, v_send, v_recv,
+    line_buf, wsend, wrecv, fsend, frecv, wide, table_h, table_l, turn, coefs, rates,
+    tbuf, south_buf, north_buf,
+    line_sem, load_sem, w_send, w_recv, f_send, f_recv, edge_send, edge_recv, row_send, row_recv, v_send,
 ):
     band, me = lax.axis_index("lat"), lax.axis_index("lon")
     north, south = lax.rem(band + 1, bands), lax.rem(band + bands - 1, bands)
@@ -142,6 +151,8 @@
     lax.fori_loop(1, sectors, greet, 0)
     for other in (north, south):
         pl.semaphore_signal(barrier, inc=1, device_id=(other, me), device_id_type=MESH)
+    pl.semaphore_signal(barrier, inc=1, device_id=(north, 1), device_id_type=MESH)
+    pl.semaphore_signal(barrier, inc=1, device_id=(south, sectors - 1), device_id_type=MESH)
 
     unit_row = lax.div(me, 2)
     line = jnp.minimum(band * rows + unit_row, FILTER_ROWS - 1)
@@ -160,7 +171,7 @@
         g = jnp.zeros((8, 128), jnp.float32)
         for mode in range(8):
             here = lax.div(lane, LEV) == mode
-            c = jnp.where(here, 0.5 * coag_ref[8 * half + mode], c)
+            c = jnp.where(here, coag_ref[8 * half + mode], c)
             g = jnp.where(here, growth_ref[8 * half + mode], g)
         rates[0, half] = c
         rates[1, half] = g
@@ -180,10 +191,12 @@
             parts.append(pltpu.roll(jnp.broadcast_to(values, (64, 128)), 64 * side, 1, stride=1, stride_axis=0))
         left = lax.broadcasted_iota(jnp.int32, (64, 128), 1) < 64
         high, rest = split_two(jnp.where(left, parts[0], parts[1]))
-        table_h[64 * k : 64 * k + 64, :] = high
-        table_l[64 * k : 64 * k + 64, :] = rest
-
-    pl.semaphore_wait(barrier, sectors + 1)
+        for at, lanes in ((64 * k, 0), (64 * ((k + 2) % sectors), 128)):
+            table_h[at : at + 64, lanes : lanes + 128] = high
+            table_l[at : at + 64, lanes : lanes + 128] = rest
+
+    extra = jnp.where(jnp.logical_or(me == 1, me == sectors - 1), sectors, 0)
+    pl.semaphore_wait(barrier, sectors + 1 + extra)
 
     def wind_copy(k):
         other = lax.rem(me + k, sectors)
@@ -208,17 +221,27 @@
             src_ref=tracers_ref.at[0], dst_ref=tbuf.at[cols + 1], send_sem=edge_send.at[1], recv_sem=edge_recv.at[1],
             device_id=(band, west), device_id_type=MESH,
         ),
-        pltpu.make_async_remote_copy(
-            src_ref=tracers_ref.at[:, pl.ds(rows - 1, 1), :], dst_ref=south_buf, send_sem=edge_send.at[2],
-            recv_sem=edge_recv.at[2], device_id=(north, me), device_id_type=MESH,
-        ),
-        pltpu.make_async_remote_copy(
-            src_ref=tracers_ref.at[:, pl.ds(0, 1), :], dst_ref=north_buf, send_sem=edge_send.at[3],
-            recv_sem=edge_recv.at[3], device_id=(south, me), device_id_type=MESH,
-        ),
     ]
     for copy in edges:
         copy.start()
+
+    groups = GROUPS
+    size = cols // groups
+
+    def row_copies(g):
+        here = pl.ds(g * size, size)
+        return [
+            pltpu.make_async_remote_copy(
+                src_ref=tracers_ref.at[here, pl.ds(row, 1), :], dst_ref=dst.at[here], send_sem=row_send.at[side, g],
+                recv_sem=row_recv.at[side, g], device_id=(target, me), device_id_type=MESH,
+            )
+            for side, (row, dst, target) in enumerate(((rows - 1, south_buf, north), (0, north_buf, south)))
+        ]
+
+    @pl.loop(0, groups)
+    def _(g):
+        for copy in row_copies(g):
+            copy.start()
 
     def wind_wait(k, carry):
         other = lax.rem(me + k, sectors)
@@ -230,58 +253,70 @@
 
     lax.fori_loop(1, sectors, wind_wait, 0)
 
-    pairs = sectors // 2
+    pairs, quads = sectors // 2, sectors // 4
     for q in range(pairs):
         one, two = wrecv[2 * q], wrecv[2 * q + 1]
         block = jnp.concatenate(
             [jnp.where(low, one, pltpu.roll(two, 64, 1)), jnp.where(low, pltpu.roll(one, 64, 1), two)], axis=0
         )
         high, rest = split_two(block)
-        for p in range(pairs):
-            at = 128 * ((q - p) % pairs)
-            wide_h[16 * p : 16 * p + 16, at : at + 128] = high
-            wide_l[16 * p : 16 * p + 16, at : at + 128] = rest
-    dot = functools.partial(jnp.dot, preferred_element_type=jnp.float32)
-    smooth = dot(wide_h[...], table_h[...]) + (dot(wide_l[...], table_h[...]) + dot(wide_h[...], table_l[...]))
+        for p in range(quads):
+            at = 128 * ((q - 2 * p) % pairs)
+            wide[16 * p : 16 * p + 16, at : at + 128] = high
+            wide[16 * (quads + p) : 16 * (quads + p) + 16, at : at + 128] = rest
+    both = jnp.dot(wide[...], table_h[...], preferred_element_type=jnp.float32)
+    rest = jnp.dot(wide[0 : 16 * quads, :], table_l[...], preferred_element_type=jnp.float32)
+    smooth = both[0 : 16 * quads] + (both[16 * quads :] + rest)
     for p in range(pairs):
-        one, two = smooth[16 * p : 16 * p + 8, :], smooth[16 * p + 8 : 16 * p + 16, :]
+        at, lanes = 16 * (p // 2), 128 * (p % 2)
+        one, two = smooth[at : at + 8, lanes : lanes + 128], smooth[at + 8 : at + 16, lanes : lanes + 128]
         fsend[2 * p] = jnp.where(low, one, pltpu.roll(two, 64, 1))
         fsend[2 * p + 1] = jnp.where(low, pltpu.roll(one, 64, 1), two)
 
-    def back_start(k, carry):
+    units = 2 * rows
+    last_unit = units - 1
+
+    def back_copy(k):
         other = lax.rem(me + k, sectors)
-        pltpu.make_async_remote_copy(
+        return pltpu.make_async_remote_copy(
             src_ref=fsend.at[other], dst_ref=frecv.at[me], send_sem=f_send.at[other], recv_sem=f_recv.at[me],
             device_id=(band, other), device_id_type=MESH,
-        ).start()
-        return carry
-
-    lax.fori_loop(1, sectors, back_start, 0)
+        )
+
+    def beyond_copy(k, slot, target):
+        other = lax.rem(me + k, sectors)
+        return pltpu.make_async_remote_copy(
+            src_ref=fsend.at[other], dst_ref=frecv.at[slot], send_sem=v_send.at[other], recv_sem=f_recv.at[slot],
+            device_id=(target, other), device_id_type=MESH,
+        )
+
+    def each(start, body):
+        def step(k, carry):
+            body(k)
+            return carry
+
+        lax.fori_loop(start, sectors, step, 0)
+
+    @pl.when(me == last_unit)
+    def _():
+        each(0, lambda k: beyond_copy(k, units, north).start())
+
+    @pl.when(me == 1)
+    def _():
+        each(0, lambda k: beyond_copy(k, units + 1, south).start())
+
+    each(1, lambda k: back_copy(k).start())
     frecv[me] = fsend[me]
 
-    def back_wait(k, carry):
-        other = lax.rem(me + k, sectors)
+    def arrived(slot):
         pltpu.make_async_remote_copy(
-            src_ref=fsend.at[me], dst_ref=frecv.at[other], send_sem=f_send.at[other], recv_sem=f_recv.at[other],
-            device_id=(band, other), device_id_type=MESH,
+            src_ref=fsend.at[me], dst_ref=frecv.at[slot], send_sem=f_send.at[me], recv_sem=f_recv.at[slot],
+            device_id=(band, east), device_id_type=MESH,
         ).wait_recv()
-        return carry
-
-    lax.fori_loop(1, sectors, back_wait, 0)
-
-    units = 2 * rows
-    to_north = pltpu.make_async_remote_copy(
-        src_ref=frecv.at[units - 1], dst_ref=frecv.at[units], send_sem=v_send.at[0], recv_sem=v_recv.at[0],
-        device_id=(north, me), device_id_type=MESH,
-    )
-    to_south = pltpu.make_async_remote_copy(
-        src_ref=frecv.at[1], dst_ref=frecv.at[units + 1], send_sem=v_send.at[1], recv_sem=v_recv.at[1],
-        device_id=(south, me), device_id_type=MESH,
-    )
-    to_north.start()
-    to_south.start()
-    to_north.wait()
-    to_south.wait()
+
+    each(1, lambda k: arrived(lax.rem(me + k, sectors)))
+    arrived(units)
+    arrived(units + 1)
 
     zero = jnp.zeros((8, 128), jnp.float32)
     merid = [frecv[units]] + [frecv[2 * r + 1] for r in range(rows)] + [frecv[units + 1]]
@@ -308,7 +343,7 @@
 
     load.wait()
     for copy in edges:
-        copy.wait()
+        copy.wait_recv()
 
     own = lax.div(lane, LEV) == sub
 
@@ -343,28 +378,33 @@
             for o in range(octets):
                 updated = moment_sources(advected[o], rates[0, part], rates[1, part])
                 for k in range(MOMENTS):
-                    obuf[j, 8 * o : 8 * o + 8, pl.ds(k * modes_width + part * 128, 128)] = updated[k]
-        pltpu.make_async_copy(obuf.at[j], out_ref.at[j], store_sem.at[j]).start()
+                    out_ref[j, 8 * o : 8 * o + 8, pl.ds(k * modes_width + part * 128, 128)] = updated[k]
         return carry
 
-    lax.fori_loop(0, cols, column, 0)
-
-    def store_wait(j, carry):
-        pltpu.make_async_copy(obuf.at[j], out_ref.at[j], store_sem.at[j]).wait()
-        return carry
-
-    lax.fori_loop(0, cols, store_wait, 0)
-
-    def send_wait(k, carry):
-        other = lax.rem(me + k, sectors)
-        wind_copy(k).wait_send()
-        pltpu.make_async_remote_copy(
-            src_ref=fsend.at[other], dst_ref=frecv.at[me], send_sem=f_send.at[other], recv_sem=f_recv.at[me],
-            device_id=(band, other), device_id_type=MESH,
-        ).wait_send()
-        return carry
-
-    lax.fori_loop(1, sectors, send_wait, 0)
+    @pl.loop(0, groups)
+    def _(g):
+        for copy in row_copies(g):
+            copy.wait_recv()
+        lax.fori_loop(g * size, g * size + size, column, 0)
+
+    each(1, lambda k: wind_copy(k).wait_send())
+    each(1, lambda k: back_copy(k).wait_send())
+
+    @pl.when(me == last_unit)
+    def _():
+        each(0, lambda k: beyond_copy(k, units, north).wait_send())
+
+    @pl.when(me == 1)
+    def _():
+        each(0, lambda k: beyond_copy(k, units + 1, south).wait_send())
+
+    for copy in edges:
+        copy.wait_send()
+
+    @pl.loop(0, groups)
+    def _(g):
+        for copy in row_copies(g):
+            copy.wait_send()
 
 
 def local(bands, sectors, tracers, winds, row_mask, coag_rate, growth_rate):
@@ -372,13 +412,13 @@
     lines = jnp.asarray(filter_lines(sectors, cols))
     f32, bf16 = jnp.float32, jnp.bfloat16
     dma = pltpu.SemaphoreType.DMA
-    anywhere = pl.BlockSpec(memory_space=pl.ANY)
+    anywhere = pl.BlockSpec(memory_space=pltpu.HBM)
     scalars = pl.BlockSpec(memory_space=pltpu.SMEM)
     out = pl.pallas_call(
         functools.partial(kernel, bands, sectors),
-        out_shape=jax.ShapeDtypeStruct((cols, rows, width), f32),
+        out_shape=pltpu.VMEM((cols, rows, width), f32),
         in_specs=[anywhere, scalars, scalars, scalars, pl.BlockSpec(memory_space=pltpu.VMEM), anywhere],
-        out_specs=anywhere,
+        out_specs=pl.BlockSpec(memory_space=pltpu.VMEM),
         scratch_shapes=[
             pltpu.VMEM((sectors, 128), f32),
             pltpu.VMEM((sectors, 8, 128), f32),
@@ -386,21 +426,19 @@
             pltpu.VMEM((sectors, 8, 128), f32),
             pltpu.VMEM((sectors + 2, 8, 128), f32),
             pltpu.VMEM((8 * sectors, 64 * sectors), bf16),
-            pltpu.VMEM((8 * sectors, 64 * sectors), bf16),
-            pltpu.VMEM((64 * sectors, 128), bf16),
-            pltpu.VMEM((64 * sectors, 128), bf16),
+            pltpu.VMEM((64 * sectors, 256), bf16),
+            pltpu.VMEM((64 * sectors, 256), bf16),
             pltpu.VMEM((3, rows // 8, 128, 128), f32),
             pltpu.VMEM((3, rows // 8, 128, 128), f32),
             pltpu.VMEM((2, 2, 8, 128), f32),
             pltpu.VMEM((cols + 2, rows, width), f32),
-            pltpu.VMEM((cols, rows, width), f32),
             pltpu.VMEM((cols, 1, width), f32),
             pltpu.VMEM((cols, 1, width), f32),
-            dma, dma, dma((cols,)),
-            dma((sectors,)), dma((sectors,)), dma((sectors,)), dma((sectors,)),
-            dma((4,)), dma((4,)), dma((2,)), dma((2,)),
+            dma, dma,
+            dma((sectors,)), dma((sectors,)), dma((sectors,)), dma((sectors + 2,)),
+            dma((2,)), dma((2,)), dma((2, GROUPS)), dma((2, GROUPS)), dma((sectors,)),
         ],
-        compiler_params=pltpu.CompilerParams(collective_id=0, has_side_effects=True),
+        compiler_params=pltpu.CompilerParams(collective_id=0, has_side_effects=True, vmem_limit_bytes=67043328 - 4 * cols * rows * width),
         name="transport",
     )(lines, row_mask, coag_rate, growth_rate, jnp.transpose(winds, (0, 2, 1)), jnp.transpose(tracers, (1, 0, 2)))
     return jnp.transpose(out, (1, 0, 2))

time: 63 us -> 54.7 us (0.87)
  Pallas kernels: 58 us -> 52.4 us
  local copies, waits for them, and re-layouts: 4.88 us -> 2.09 us
    pallas_call x1, Pallas kernels: 58 us -> 52.4 us  [local(): pl.pallas_call(functools.partial(kernel, bands, sectors), out_shape=pltpu...]
    unnamed x1, local copies, waits for them, and re-layouts: 4.88 us -> 2.09 us
where the time goes in v2:
time: 54.7 us; the launch traced here: 54.5 us
  Pallas kernels  52.4 us (96%)
  local copies, waits for them, and re-layouts  2.09 us (4%)
    pallas_call x1, Pallas kernels, local(): pl.pallas_call(functools.partial(kernel, bands, sectors), out_shape=pltpu...  52.4 us
    unnamed x1, local copies, waits for them, and re-layouts  2.09 us

profile of v2, /device:TPU:1, one launch (start us, length us, event | category | flops | bytes accessed | tf_op | source)
XLA Modules:
  0.0 54.5 jit_solution(12894422220157984818)
XLA Ops:
  0.0 52.4 %transport.1 = f32[45,16,1536]{2,1,0:T(8,128)S(1)} custom-call(f32[48,32,128]{2,1,0:T(8,128)} %constant.2.clone.lines_ref, s32[16]{0:T(128)} %mask_ref.1, f32[16]{0:T(128)} %coag_ref.1, f32[16]{0:T(128)} %growth_ref.1, f32[16,32,45]{2,1,0:T(8,128)} %bitcast.5, f32[45,16,1536]{2,1,0:T(8,128)} %bitcast.4), custom_call_target="tpu_custom_call" | custom-call | tf_op jit(solution)/shard_map/transport/pallas_call | solution.py:417
  52.4 2.1 %copy.8 = f32[16,45,1536]{2,0,1:T(8,128)} copy(f32[16,45,1536]{2,0,1:T(8,128)S(1)} %bitcast.3) | data formatting | bytes 8847360

commit v3 on v2

--- a/solution.py
+++ b/solution.py
@@ -15,7 +15,7 @@
 MODES = 16
 MOMENTS = 6
 FILTER_ROWS = 48
-GROUPS = 5
+GROUP = 4
 MESH = pl.DeviceIdType.MESH
 
 POLY = (
@@ -129,7 +129,7 @@
 def kernel(
     bands, sectors, lines_ref, mask_ref, coag_ref, growth_ref, winds_ref, tracers_ref, out_ref,
     line_buf, wsend, wrecv, fsend, frecv, wide, table_h, table_l, turn, coefs, rates,
-    tbuf, south_buf, north_buf,
+    tbuf, south_buf, north_buf, even, odd,
     line_sem, load_sem, w_send, w_recv, f_send, f_recv, edge_send, edge_recv, row_send, row_recv, v_send,
 ):
     band, me = lax.axis_index("lat"), lax.axis_index("lon")
@@ -225,22 +225,27 @@
     for copy in edges:
         copy.start()
 
-    groups = GROUPS
-    size = cols // groups
-
-    def row_copies(g):
-        here = pl.ds(g * size, size)
+    groups = (cols - 1) // GROUP
+
+    def row_copies(slot, start, size):
+        here = pl.ds(start, size)
         return [
             pltpu.make_async_remote_copy(
-                src_ref=tracers_ref.at[here, pl.ds(row, 1), :], dst_ref=dst.at[here], send_sem=row_send.at[side, g],
-                recv_sem=row_recv.at[side, g], device_id=(target, me), device_id_type=MESH,
+                src_ref=tracers_ref.at[here, pl.ds(row, 1), :], dst_ref=dst.at[here], send_sem=row_send.at[side, slot],
+                recv_sem=row_recv.at[side, slot], device_id=(target, me), device_id_type=MESH,
             )
             for side, (row, dst, target) in enumerate(((rows - 1, south_buf, north), (0, north_buf, south)))
         ]
 
+    def group_copies(g):
+        return row_copies(g, GROUP * g + 1, GROUP)
+
+    for copy in row_copies(groups, 0, 1):
+        copy.start()
+
     @pl.loop(0, groups)
     def _(g):
-        for copy in row_copies(g):
+        for copy in group_copies(g):
             copy.start()
 
     def wind_wait(k, carry):
@@ -356,11 +361,12 @@
 
     modes_width = width // MOMENTS
 
-    def column(j, carry):
+    parts = modes_width // 128
+
+    def advect(j, buf):
         places = [(0, j), (0, 64 + j), (1, j), (1, 64 + j), (2, j)]
         stencil = [[expand(n, octet, place) for n, place in places] for octet in range(octets)]
-        for part in range(modes_width // 128):
-            advected = [[] for _ in range(octets)]
+        for part in range(parts):
             for k in range(MOMENTS):
                 lanes = pl.ds(k * modes_width + part * 128, 128)
                 q = [tbuf[j + 1, 8 * o : 8 * o + 8, lanes] for o in range(octets)]
@@ -374,18 +380,29 @@
                     below = jnp.where(sub > 0, up[o + 1], up[o])
                     octet_rows = pl.ds(8 * o, 8)
                     value = c * q[o] + ce * tbuf[j + 2, octet_rows, lanes] + cw * tbuf[j, octet_rows, lanes]
-                    advected[o].append(value + cn * above + cs * below)
+                    buf[part, o, k] = value + cn * above + cs * below
+
+    def produce(j, buf):
+        for part in range(parts):
             for o in range(octets):
-                updated = moment_sources(advected[o], rates[0, part], rates[1, part])
-                for k in range(MOMENTS):
-                    out_ref[j, 8 * o : 8 * o + 8, pl.ds(k * modes_width + part * 128, 128)] = updated[k]
-        return carry
+                moments = [buf[part, o, k] for k in range(MOMENTS)]
+                for k, value in enumerate(moment_sources(moments, rates[0, part], rates[1, part])):
+                    out_ref[j, 8 * o : 8 * o + 8, pl.ds(k * modes_width + part * 128, 128)] = value
+
+    for copy in row_copies(groups, 0, 1):
+        copy.wait_recv()
+    advect(0, even)
 
     @pl.loop(0, groups)
     def _(g):
-        for copy in row_copies(g):
+        for copy in group_copies(g):
             copy.wait_recv()
-        lax.fori_loop(g * size, g * size + size, column, 0)
+        for k in range(GROUP):
+            now, later = (even, odd) if k % 2 == 0 else (odd, even)
+            advect(GROUP * g + k + 1, later)
+            produce(GROUP * g + k, now)
+
+    produce(cols - 1, even)
 
     each(1, lambda k: wind_copy(k).wait_send())
     each(1, lambda k: back_copy(k).wait_send())
@@ -401,9 +418,12 @@
     for copy in edges:
         copy.wait_send()
 
+    for copy in row_copies(groups, 0, 1):
+        copy.wait_send()
+
     @pl.loop(0, groups)
     def _(g):
-        for copy in row_copies(g):
+        for copy in group_copies(g):
             copy.wait_send()
 
 
@@ -412,6 +432,8 @@
     lines = jnp.asarray(filter_lines(sectors, cols))
     f32, bf16 = jnp.float32, jnp.bfloat16
     dma = pltpu.SemaphoreType.DMA
+    groups = (cols - 1) // GROUP
+    stage = (width // MOMENTS // 128, rows // 8, MOMENTS, 8, 128)
     anywhere = pl.BlockSpec(memory_space=pltpu.HBM)
     scalars = pl.BlockSpec(memory_space=pltpu.SMEM)
     out = pl.pallas_call(
@@ -434,9 +456,11 @@
             pltpu.VMEM((cols + 2, rows, width), f32),
             pltpu.VMEM((cols, 1, width), f32),
             pltpu.VMEM((cols, 1, width), f32),
+            pltpu.VMEM(stage, f32),
+            pltpu.VMEM(stage, f32),
             dma, dma,
             dma((sectors,)), dma((sectors,)), dma((sectors,)), dma((sectors + 2,)),
-            dma((2,)), dma((2,)), dma((2, GROUPS)), dma((2, GROUPS)), dma((sectors,)),
+            dma((2,)), dma((2,)), dma((2, groups + 1)), dma((2, groups + 1)), dma((sectors,)),
         ],
         compiler_params=pltpu.CompilerParams(collective_id=0, has_side_effects=True, vmem_limit_bytes=67043328 - 4 * cols * rows * width),
         name="transport",

time: 54.7 us -> 47.3 us (0.86)
  Pallas kernels: 52.4 us -> 45 us
    pallas_call x1, Pallas kernels: 52.4 us -> 45 us  [local(): pl.pallas_call(functools.partial(kernel, bands, sectors), out_shape=pltpu...]
where the time goes in v3:
time: 47.3 us; the launch traced here: 47.1 us
  Pallas kernels  45 us (95%)
  local copies, waits for them, and re-layouts  2.09 us (4%)
    pallas_call x1, Pallas kernels, local(): pl.pallas_call(functools.partial(kernel, bands, sectors), out_shape=pltpu...  45 us
    unnamed x1, local copies, waits for them, and re-layouts  2.09 us

profile of v3, /device:TPU:1, one launch (start us, length us, event | category | flops | bytes accessed | tf_op | source)
XLA Modules:
  0.0 47.1 jit_solution(894945915593952575)
XLA Ops:
  0.0 45.0 %transport.1 = f32[45,16,1536]{2,1,0:T(8,128)S(1)} custom-call(f32[48,32,128]{2,1,0:T(8,128)} %constant.2.clone.lines_ref, s32[16]{0:T(128)} %mask_ref.1, f32[16]{0:T(128)} %coag_ref.1, f32[16]{0:T(128)} %growth_ref.1, f32[16,32,45]{2,1,0:T(8,128)} %bitcast.5, f32[45,16,1536]{2,1,0:T(8,128)} %bitcast.4), custom_call_target="tpu_custom_call" | custom-call | tf_op jit(solution)/shard_map/transport/pallas_call | solution.py:439
  45.0 2.1 %copy.8 = f32[16,45,1536]{2,0,1:T(8,128)} copy(f32[16,45,1536]{2,0,1:T(8,128)S(1)} %bitcast.3) | data formatting | bytes 8847360

commit v4 on v3

--- a/solution.py
+++ b/solution.py
@@ -209,7 +209,8 @@
         wind_copy(k).start()
         return carry
 
-    lax.fori_loop(1, sectors, wind_start, 0)
+    for k in sorted(range(1, sectors), key=lambda k: abs(k % 16 - 8)):
+        wind_copy(k).start()
     wrecv[me] = wsend[me]
 
     edges = [
@@ -239,14 +240,6 @@
 
     def group_copies(g):
         return row_copies(g, GROUP * g + 1, GROUP)
-
-    for copy in row_copies(groups, 0, 1):
-        copy.start()
-
-    @pl.loop(0, groups)
-    def _(g):
-        for copy in group_copies(g):
-            copy.start()
 
     def wind_wait(k, carry):
         other = lax.rem(me + k, sectors)
@@ -310,8 +303,18 @@
     def _():
         each(0, lambda k: beyond_copy(k, units + 1, south).start())
 
-    each(1, lambda k: back_copy(k).start())
+    for k in sorted(range(1, sectors), key=lambda k: abs(k % 16 - 8)):
+        back_copy(k).start()
     frecv[me] = fsend[me]
+
+    for copy in row_copies(groups, 0, 1):
+        copy.start()
+
+    @pl.loop(0, groups)
+    def _(g):
+        for copy in group_copies(g):
+            copy.start()
+
 
     def arrived(slot):
         pltpu.make_async_remote_copy(
@@ -399,8 +402,8 @@
             copy.wait_recv()
         for k in range(GROUP):
             now, later = (even, odd) if k % 2 == 0 else (odd, even)
+            produce(GROUP * g + k, now)
             advect(GROUP * g + k + 1, later)
-            produce(GROUP * g + k, now)
 
     produce(cols - 1, even)
 

time: 47.3 us -> 45.1 us (0.953)
  Pallas kernels: 45 us -> 42.7 us
    pallas_call x1, Pallas kernels: 45 us -> 42.7 us  [local(): pl.pallas_call(functools.partial(kernel, bands, sectors), out_shape=pltpu...]
where the time goes in v4:
time: 45.1 us; the launch traced here: 44.8 us
  Pallas kernels  42.7 us (95%)
  local copies, waits for them, and re-layouts  2.09 us (5%)
    pallas_call x1, Pallas kernels, local(): pl.pallas_call(functools.partial(kernel, bands, sectors), out_shape=pltpu...  42.7 us
    unnamed x1, local copies, waits for them, and re-layouts  2.09 us

profile of v4, /device:TPU:1, one launch (start us, length us, event | category | flops | bytes accessed | tf_op | source)
XLA Modules:
  0.0 44.8 jit_solution(4122076597417375151)
XLA Ops:
  0.0 42.7 %transport.1 = f32[45,16,1536]{2,1,0:T(8,128)S(1)} custom-call(f32[48,32,128]{2,1,0:T(8,128)} %constant.2.clone.lines_ref, s32[16]{0:T(128)} %mask_ref.1, f32[16]{0:T(128)} %coag_ref.1, f32[16]{0:T(128)} %growth_ref.1, f32[16,32,45]{2,1,0:T(8,128)} %bitcast.5, f32[45,16,1536]{2,1,0:T(8,128)} %bitcast.4), custom_call_target="tpu_custom_call" | custom-call | tf_op jit(solution)/shard_map/transport/pallas_call | solution.py:442
  42.7 2.1 %copy.8 = f32[16,45,1536]{2,0,1:T(8,128)} copy(f32[16,45,1536]{2,0,1:T(8,128)S(1)} %bitcast.3) | data formatting | bytes 8847360

commit v5 on v4

--- a/solution.py
+++ b/solution.py
@@ -86,14 +86,13 @@
     rest = c - along
     ys = (c + (along + along), rest + across, rest - across)
     xs = [y + a0 for y in ys]
-    gaps = (ys[0] - ys[1], ys[0] - ys[2], ys[1] - ys[2])
-    dens = (gaps[0] * gaps[1], -gaps[0] * gaps[2], gaps[1] * gaps[2])
-    ws, shares = [], []
-    for i, j, k in ((0, 1, 2), (1, 0, 2), (2, 0, 1)):
-        above = 1.0 + xs[i]
-        share = (s1 + m0 * (ys[j] * ys[k])) / (dens[i] * above)
-        ws.append(share * above)
-        shares.append(share)
+    above = [1.0 + x for x in xs]
+    wide = ys[0] - ys[2]
+    top = (s1 + m0 * (ys[1] * ys[2])) / ((ys[0] - ys[1]) * (wide * above[0]))
+    low = (s1 + m0 * (ys[0] * ys[1])) / ((ys[1] - ys[2]) * (wide * above[2]))
+    w_top, w_low = top * above[0], low * above[2]
+    w_mid = m0 - (w_top + w_low)
+    ws, shares = (w_top, w_mid, w_low), (top, w_mid / above[1], low)
     vs = [x * x * x for x in xs]
     cw = [w * coag for w in ws]
     wv = [ws[i] * vs[i] for i in range(3)]
@@ -104,7 +103,7 @@
     pairs, roots, joins = [], [], []
     for i, j in ((0, 1), (0, 2), (1, 2)):
         joined = vs[i] + vs[j]
-        roots.append(jnp.exp2(jnp.log(joined) * (math.log2(math.e) / 3.0)))
+        roots.append(jnp.exp(jnp.log(joined) * (1.0 / 3.0)))
         pairs.append(cw[i] * ws[j] * joined)
         joins.append(joined)
     cm0, cm3 = coag * m0, coag * m3
@@ -114,7 +113,7 @@
     for k in range(1, MOMENTS):
         pairs = [pairs[i] * roots[i] for i in range(3)]
         diag = [diag[i] * xs[i] for i in range(3)]
-        total = moments[k] + (float(k) * growth) * grown
+        total = moments[k] + growth[k - 1] * grown
         grown = moments[k - 1] - grown
         if k == 3:
             left = [pairs[i] - first[i] * joins[i] for i in range(3)]
@@ -174,7 +173,8 @@
             c = jnp.where(here, coag_ref[8 * half + mode], c)
             g = jnp.where(here, growth_ref[8 * half + mode], g)
         rates[0, half] = c
-        rates[1, half] = g
+        for k in range(1, MOMENTS):
+            rates[k, half] = float(k) * g
 
     line_copy.wait()
     filtered = mask_ref[unit_row] > 0
@@ -389,7 +389,7 @@
         for part in range(parts):
             for o in range(octets):
                 moments = [buf[part, o, k] for k in range(MOMENTS)]
-                for k, value in enumerate(moment_sources(moments, rates[0, part], rates[1, part])):
+                for k, value in enumerate(moment_sources(moments, rates[0, part], [rates[k, part] for k in range(1, MOMENTS)])):
                     out_ref[j, 8 * o : 8 * o + 8, pl.ds(k * modes_width + part * 128, 128)] = value
 
     for copy in row_copies(groups, 0, 1):
@@ -455,7 +455,7 @@
             pltpu.VMEM((64 * sectors, 256), bf16),
             pltpu.VMEM((3, rows // 8, 128, 128), f32),
             pltpu.VMEM((3, rows // 8, 128, 128), f32),
-            pltpu.VMEM((2, 2, 8, 128), f32),
+            pltpu.VMEM((MOMENTS, 2, 8, 128), f32),
             pltpu.VMEM((cols + 2, rows, width), f32),
             pltpu.VMEM((cols, 1, width), f32),
             pltpu.VMEM((cols, 1, width), f32),

time: 45.1 us -> 45 us (level)
  no operation moved by 1% of the time
where the time goes in v5:
time: 45 us; the launch traced here: 44.7 us
  Pallas kernels  42.6 us (95%)
  local copies, waits for them, and re-layouts  2.09 us (5%)
    pallas_call x1, Pallas kernels, local(): pl.pallas_call(functools.partial(kernel, bands, sectors), out_shape=pltpu...  42.6 us
    unnamed x1, local copies, waits for them, and re-layouts  2.09 us

profile of v5, /device:TPU:1, one launch (start us, length us, event | category | flops | bytes accessed | tf_op | source)
XLA Modules:
  0.0 44.7 jit_solution(1240077158414393804)
XLA Ops:
  0.0 42.6 %transport.1 = f32[45,16,1536]{2,1,0:T(8,128)S(1)} custom-call(f32[48,32,128]{2,1,0:T(8,128)} %constant.2.clone.lines_ref, s32[16]{0:T(128)} %mask_ref.1, f32[16]{0:T(128)} %coag_ref.1, f32[16]{0:T(128)} %growth_ref.1, f32[16,32,45]{2,1,0:T(8,128)} %bitcast.5, f32[45,16,1536]{2,1,0:T(8,128)} %bitcast.4), custom_call_target="tpu_custom_call" | custom-call | tf_op jit(solution)/shard_map/transport/pallas_call | solution.py:442
  42.6 2.1 %copy.8 = f32[16,45,1536]{2,0,1:T(8,128)} copy(f32[16,45,1536]{2,0,1:T(8,128)S(1)} %bitcast.3) | data formatting | bytes 8847360
